TPU v7x, 256 devices: a whole 4x4x8 slice. The times are simulated.
256 devices in a mesh: dp: 16 (over y, x), expert: 16 (over z, core).
Axes of the slice: x: 4, y: 4, z: 8, core: 2. Of those that a mesh axis runs over, the one named last changes fastest.
Arguments:
- tokens: float32 [2048, 2048], P('expert'), may hold values from -6 to 6
- expert_ids: int32 [2048, 8], P('expert'), may hold values from 0 to 127, all different within a row; in each aligned block of 128 rows (0 to 127, 128 to 255, ...) at most 10 rows name the same one
- gate_values: float32 [2048, 8], P('expert'), may hold values from 0.05 to 1
- valid_mask: int32 [2048], P('expert'), may hold values from 0 to 1, as said below
- gate_weight: bfloat16 [128, 1536, 2048], P('expert', 'dp'), may hold values from -0.125 to 0.125
- up_weight: bfloat16 [128, 1536, 2048], P('expert', 'dp'), may hold values from -0.125 to 0.125
- down_weight: bfloat16 [128, 1536, 2048], P('expert', 'dp'), may hold values from -0.15625 to 0.15625
Outputs:
- blended: float32 [2048, 2048], P('expert')
- loss: float32 [], replicated
Inputs may be any that keep to these rules, and one draw needn't show every extreme that they name: `expert_ids`: each row names 8 different experts; in the 128 rows of one block no expert is named more than 10 times. `valid_mask`: each block of 128 tokens holds at least one valid token.
All inputs are finite; a program needn't handle non-finite values.
Results may differ from a plain program's by a relative error of at most 0.0058.
Values may be sent and summed in bfloat16 or wider, within the bound.
A program may use at most 128 MiB of HBM per device.

v0:
```python
import jax
import jax.numpy as jnp
from jax import lax
from jax.sharding import PartitionSpec as P

SLOTS = 16


def on_device(tokens, expert_ids, gate_values, valid_mask, gate_weight, up_weight, down_weight):
    tok_count, width = tokens.shape
    local_experts = gate_weight.shape[0]
    blocks = lax.axis_size("expert")
    parts = lax.axis_size("dp")
    piece = width // parts
    me = lax.axis_index("expert")
    part = lax.axis_index("dp")
    weights = valid_mask.astype(jnp.float32)
    mine = lax.dynamic_slice(tokens, (0, part * piece), (tok_count, piece)).astype(jnp.bfloat16)
    column = lax.all_gather(mine, "expert", axis=0, tiled=True)
    every = lax.all_gather(column, "dp", axis=1, tiled=True)
    ids = lax.all_gather(expert_ids, "expert", axis=0, tiled=True)
    gates = lax.all_gather(gate_values * weights[:, None], "expert", axis=0, tiled=True)
    local = me * local_experts + jnp.arange(local_experts, dtype=jnp.int32)
    match = ids[:, None, :] == local[None, :, None]
    named = jnp.any(match, axis=2)
    gate = jnp.sum(jnp.where(match, gates[:, None, :], 0.0), axis=2).reshape(
        blocks, tok_count, local_experts
    )
    taken = named.astype(jnp.int32).reshape(blocks, tok_count, local_experts)
    rank = jnp.cumsum(taken, axis=1) - taken
    pick = (
        rank.transpose(0, 2, 1)[:, :, None, :]
        == jnp.arange(SLOTS, dtype=jnp.int32)[None, None, :, None]
    ) & (taken.transpose(0, 2, 1)[:, :, None, :] > 0)
    slot_gate = jnp.sum(jnp.where(pick, gate.transpose(0, 2, 1)[:, :, None, :], 0.0), axis=3)
    pick = pick.astype(jnp.bfloat16)
    rows = jnp.einsum(
        "best,btf->ebsf",
        pick,
        every.reshape(blocks, tok_count, width),
        preferred_element_type=jnp.float32,
    ).astype(jnp.bfloat16)
    rows = rows.reshape(local_experts, blocks * SLOTS, width)
    gate_pre = jnp.einsum("erd,efd->erf", rows, gate_weight, preferred_element_type=jnp.float32)
    up_pre = jnp.einsum("erd,efd->erf", rows, up_weight, preferred_element_type=jnp.float32)
    hidden = (jax.nn.silu(gate_pre) * up_pre).astype(jnp.bfloat16)
    out = jnp.einsum("erf,efd->erd", hidden, down_weight, preferred_element_type=jnp.float32)
    out = (
        out.reshape(local_experts, blocks, SLOTS, width)
        * slot_gate.transpose(1, 0, 2)[:, :, :, None]
    )
    mixed = jnp.einsum(
        "best,ebsf->btf", pick, out.astype(jnp.bfloat16), preferred_element_type=jnp.float32
    ).reshape(blocks * tok_count, width)
    summed = lax.psum_scatter(mixed.astype(jnp.bfloat16), "dp", scatter_dimension=1, tiled=True)
    own = lax.psum_scatter(summed.astype(jnp.float32), "expert", scatter_dimension=0, tiled=True)
    blended = lax.all_gather(own, "dp", axis=1, tiled=True)
    per_token = jnp.mean(blended * blended, axis=1)
    local_loss = jnp.sum(per_token * weights)
    loss_sum, token_total = lax.psum((local_loss, jnp.sum(weights)), "expert")
    return (blended, loss_sum / token_total)


def solution(mesh):
    return jax.shard_map(
        on_device,
        mesh=mesh,
        in_specs=(
            P("expert", None),
            P("expert", None),
            P("expert", None),
            P("expert"),
            P("expert", "dp", None),
            P("expert", "dp", None),
            P("expert", "dp", None),
        ),
        out_specs=(P("expert", None), P()),
        check_vma=False,
    )
```

profile of v0, /device:TPU:1, one launch (start us, length us, event | category | flops | bytes accessed | tf_op | source)
XLA Modules:
  0.0 415.1 jit_solution(1104938401888615248)
XLA Ops:
  7.2 0.0 all-gather.3.cloned.1.call-start
  7.2 1.0 dynamic-slice_convert_fusion
  8.2 24.1 %all_gather.16 = bf16[2048,128]{1,0:T(8,128)(2,1)} all-gather(bf16[128,128]{1,0:T(8,128)(2,1)S(1)} %dynamic-slice_convert_fusion), channel_id=1, replica_groups=mesh['dp'=16,'expert'=16] {'expert'}, dimensions={0}, use_global_device_ids=true | all-gather | bytes 557056 | tf_op jit(solution)/shard_map/all_gather | solution.py:19
  32.4 0.0 reduce-scatter.7.cloned.1.call-start
  32.4 0.7 convert_element_type.41
  33.1 14.9 %all_gather.15 = s32[2048,8]{0,1:T(8,128)S(1)} all-gather(s32[128,8]{0,1:T(8,128)} %param.8), channel_id=1, replica_groups=mesh['dp'=16,'expert'=16] {'expert'}, dimensions={0}, use_global_device_ids=true | all-gather | bytes 69632 | tf_op jit(solution)/shard_map/all_gather | solution.py:21
  47.9 0.2 compare_reduce_fusion
  48.2 1.4 copy.28
  49.6 2.8 subtract_bitcast_fusion
  52.4 1.6 copy.30
  54.0 0.7 broadcast_multiply_fusion
  54.7 15.9 %all_gather.18 = f32[2048,8]{0,1:T(8,128)S(1)} all-gather(f32[128,8]{0,1:T(8,128)S(1)} %broadcast_multiply_fusion), channel_id=1, replica_groups=mesh['dp'=16,'expert'=16] {'expert'}, dimensions={0}, use_global_device_ids=true | all-gather | bytes 69632 | tf_op jit(solution)/shard_map/all_gather | solution.py:22
  70.6 0.2 fusion.16
  70.9 0.4 select_reduce_fusion
  71.3 39.7 %all-gather.3.cloned.1.call-done = bf16[2048,2048]{1,0:T(8,128)(2,1)} async-done(((bf16[2048,128]{1,0:T(8,128)(2,1)}), bf16[2048,2048]{1,0:T(8,128)(2,1)}) %all-gather.3.cloned.1.call-update) | async-done | bytes 8388624 | tf_op jit(solution)/shard_map/all_gather | solution.py:20
  111.0 8.9 %convert_bitcast_fusion = bf16[8,16,16,2048]{3,2,0,1:T(8,128)(2,1)} fusion(bf16[16,128,2048,1]{2,1,3,0:T(8,128)(2,1)} %bitcast.42, s32[16,8,128]{2,1,0:T(8,128)S(1)} %copy.30, pred[16,8,128]{2,1,0:T(8,128)(4,1)S(1)} %compare_bitcast_fusion), kind=kOutput, calls=%fused_computation.5 | convolution fusion | flops 1078460416 | bytes 16859136 | tf_op jit(solution)/shard_map/best,btf->ebsf/dot_general | solution.py:37
  119.9 8.4 %copy.31 = bf16[8,16,16,2048]{3,2,1,0:T(8,128)(2,1)} copy(bf16[8,16,16,2048]{3,2,0,1:T(8,128)(2,1)} %convert_bitcast_fusion) | data formatting | bytes 16777216 | tf_op jit(solution)/shard_map/convert_element_type | solution.py:42
  128.3 7.0 %fusion.23 = f32[8,256,96]{1,2,0:T(8,128)} fusion(bf16[8,256,2048]{2,1,0:T(8,128)(2,1)} %bitcast.37, bf16[8,96,2048]{2,1,0:T(8,128)(2,1)S(1)} %copy-done.3), kind=kOutput, calls=%fused_computation.35 | convolution fusion | flops 805306368 | bytes 12320768 | tf_op jit(solution)/shard_map/erd,efd->erf/dot_general | solution.py:44
  135.3 15.4 %fusion.7 = f32[8,256,2048]{2,1,0:T(8,128)} fusion(bf16[8,96,2048]{2,1,0:T(8,128)(2,1)S(1)} %copy-done, bf16[8,256,2048]{2,1,0:T(8,128)(2,1)} %bitcast.38, bf16[8,96,2048]{2,1,0:T(8,128)(2,1)} %param.12, f32[8,256,96]{1,2,0:T(8,128)} %fusion.23), kind=kOutput, calls=%fused_computation.8 | convolution fusion | flops 1611792384 | bytes 32243712 | tf_op jit(solution)/shard_map/erf,efd->erd/dot_general | solution.py:47
  150.7 11.4 %bitcast_convert_fusion = bf16[16,128,2048]{2,1,0:T(8,128)(2,1)} fusion(f32[8,16,16,2048]{3,2,1,0:T(8,128)} %bitcast.34, f32[8,16,16]{2,0,1:T(8,128)S(1)} %bitcast.40, s32[16,8,128]{2,1,0:T(8,128)S(1)} %copy.30, pred[16,8,128]{2,1,0:T(8,128)(4,1)S(1)} %compare_bitcast_fusion), kind=kOutput, calls=%fused_computation | convolution fusion | flops 1086849024 | bytes 25255936 | tf_op jit(solution)/shard_map/best,ebsf->btf/dot_general | solution.py:52
  162.1 12.5 %copy.35 = bf16[2048,2048]{0,1:T(8,128)(2,1)} copy(bf16[2048,2048]{1,0:T(8,128)(2,1)} %bitcast.36) | data formatting | bytes 16777216
  174.6 0.0 reduce-scatter.5.cloned.1.call-start
  174.7 90.3 %reduce-scatter.7.cloned.1.call-done = bf16[128,2048]{1,0:T(8,128)(2,1)} async-done(((bf16[2048,2048]{1,0:T(8,128)(2,1)}), bf16[128,2048]{1,0:T(8,128)(2,1)}) %reduce-scatter.7.cloned.1.call-update) | async-done | bytes 524304
  265.0 2.0 copy.36
  267.0 2.1 convert_element_type.45
  269.1 0.0 all-gather.5.cloned.1.call-start
  269.1 56.4 %reduce-scatter.5.cloned.1.call-done = f32[128,128]{1,0:T(8,128)} async-done(((f32[2048,128]{1,0:T(8,128)}), f32[128,128]{1,0:T(8,128)}) %reduce-scatter.5.cloned.1.call-update) | async-done | bytes 65552 | tf_op jit(solution)/shard_map/reduce_scatter | solution.py:56
  325.6 50.0 %all-gather.5.cloned.1.call-done = f32[128,2048]{1,0:T(8,128)} async-done(((f32[128,128]{1,0:T(8,128)}), f32[128,2048]{1,0:T(8,128)}) %all-gather.5.cloned.1.call-update) | async-done | bytes 1048592 | tf_op jit(solution)/shard_map/all_gather | solution.py:57
  375.5 1.4 multiply_reduce_fusion
  376.9 0.6 convert_reduce_fusion
  377.5 26.3 %all-reduce = (f32[]{:T(128)}, f32[]{:T(128)}) all-reduce(f32[]{:T(128)} %get-tuple-element.3, f32[]{:T(128)} %get-tuple-element.2), channel_id=1, replica_groups=mesh['dp'=16,'expert'=16] {'expert'}, use_global_device_ids=true, to_apply=%region_8.9 | all-reduce | flops 2 | bytes 16 | tf_op jit(solution)/shard_map/psum | solution.py:60
  405.1 2.3 copy.44
  (15 shorter events, 0.1 us)
Async XLA Ops:
  7.2 128.2 %copy-start = (bf16[8,96,2048]{2,1,0:T(8,128)(2,1)S(1)}, bf16[8,96,2048]{2,1,0:T(8,128)(2,1)}, u32[]{:S(2)}) copy-start(bf16[8,96,2048]{2,1,0:T(8,128)(2,1)} %param.13) | copy-start | bytes 9437188
  7.2 103.8 %all-gather.3.cloned.1.call-start = ((), (), s32[]{:S(2)}) async-start(), calls=%async_computation.2 | async-start | bytes 8912896 | tf_op jit(solution)/shard_map/all_gather | solution.py:20
  32.4 232.6 %reduce-scatter.7.cloned.1.call-start = ((), (), s32[]{:S(2)}) async-start(), calls=%async_computation.5 | async-start | bytes 8912896
  119.9 8.4 %copy-start.3 = (bf16[8,96,2048]{2,1,0:T(8,128)(2,1)S(1)}, bf16[8,96,2048]{2,1,0:T(8,128)(2,1)}, u32[]{:S(2)}) copy-start(bf16[8,96,2048]{2,1,0:T(8,128)(2,1)} %param.11) | copy-start | bytes 9437188
  162.1 245.3 %copy-start.1 = (bf16[8,96,2048]{2,1,0:T(8,128)(2,1)S(1)}, bf16[8,96,2048]{2,1,0:T(8,128)(2,1)}, u32[]{:S(2)}) copy-start(bf16[8,96,2048]{2,1,0:T(8,128)(2,1)} %param.13) | copy-start | bytes 9437188
  174.6 202.3 %copy-start.2 = (s32[128]{0:T(128)S(1)}, s32[128]{0:T(128)}, u32[]{:S(2)}) copy-start(s32[128]{0:T(128)} %param.10) | copy-start | bytes 1540
  174.6 150.9 %reduce-scatter.5.cloned.1.call-start = ((), (), s32[]{:S(2)}) async-start(), calls=%async_computation.3 | async-start | bytes 1114112 | tf_op jit(solution)/shard_map/reduce_scatter | solution.py:56
  269.1 106.5 %all-gather.5.cloned.1.call-start = ((), (), s32[]{:S(2)}) async-start(), calls=%async_computation.4 | async-start | bytes 1114112 | tf_op jit(solution)/shard_map/all_gather | solution.py:57
Sparse Core Ops, SparseCore 0:
  32.5 78.4 all-gather.2
  174.8 90.1 reduce-scatter.6
  269.2 56.2 reduce-scatter.4
  327.8 47.6 all-gather.4
where the time goes:
time: 416 us; the launch traced here: 415 us
  waiting for transfers between devices  236 us (57%)
  blocking collectives  81.2 us (20%)
  matrix products  42.7 us (10%)
  local copies, waits for them, and re-layouts  29.2 us (7%)
  between operations  16.3 us (4%)
  other arithmetic  9.13 us (2%)
    unnamed x5, waiting for transfers between devices  90.3 us
    reduce_scatter x1, waiting for transfers between devices, on_device(): lax.psum_scatter(summed.astype(jnp.float32), 'expert', scatter_dimension=...  56.4 us
    all_gather x1, waiting for transfers between devices, on_device(): blended = lax.all_gather(own, 'dp', axis=1, tiled=True)  50 us
    all_gather x1, waiting for transfers between devices, on_device(): every = lax.all_gather(column, 'dp', axis=1, tiled=True)  39.7 us
    psum x1, blocking collectives, on_device(): loss_sum, token_total = lax.psum((local_loss, jnp.sum(weights)), 'expert')  26.3 us
    all_gather x1, blocking collectives, on_device(): column = lax.all_gather(mine, 'expert', axis=0, tiled=True)  24.1 us
    unnamed x11, local copies, waits for them, and re-layouts  16.8 us
    all_gather x1, blocking collectives, on_device(): lax.all_gather(gate_values * weights[:, None], 'expert', axis=0, tiled=True)  15.9 us
  transfers between devices with their start and end apart: 4, of which 4 were waited for; matrix products, arithmetic and copies ran while one was open for 2% of the time, Pallas kernels for 0%

commit v1 on v0

--- a/solution.py
+++ b/solution.py
@@ -4,6 +4,13 @@
 from jax.sharding import PartitionSpec as P
 
 SLOTS = 16
+
+
+def swapped_in(x, axis, dim):
+    size = lax.axis_size(axis)
+    tiles = jnp.stack([x for _ in range(size)])
+    tiles = lax.all_to_all(tiles, axis, split_axis=0, concat_axis=0)
+    return jnp.concatenate(tiles, axis=dim)
 
 
 def on_device(tokens, expert_ids, gate_values, valid_mask, gate_weight, up_weight, down_weight):
@@ -54,7 +61,7 @@
     ).reshape(blocks * tok_count, width)
     summed = lax.psum_scatter(mixed.astype(jnp.bfloat16), "dp", scatter_dimension=1, tiled=True)
     own = lax.psum_scatter(summed.astype(jnp.float32), "expert", scatter_dimension=0, tiled=True)
-    blended = lax.all_gather(own, "dp", axis=1, tiled=True)
+    blended = swapped_in(own, "dp", 1)
     per_token = jnp.mean(blended * blended, axis=1)
     local_loss = jnp.sum(per_token * weights)
     loss_sum, token_total = lax.psum((local_loss, jnp.sum(weights)), "expert")

time: 416 us -> 392 us (0.942)
  waiting for transfers between devices: 236 us -> 187 us
  blocking collectives: 81.2 us -> 104 us
    all_gather x1 -> x0, waiting for transfers between devices: 50 us -> none  [on_device(): blended = lax.all_gather(own, 'dp', axis=1, tiled=True)]
    all_to_all x0 -> x1, blocking collectives: none -> 19.7 us  [swapped_in(): tiles = lax.all_to_all(tiles, axis, split_axis=0, concat_axis=0)]
    unnamed x5 -> x4, waiting for transfers between devices: 90.3 us -> 90.3 us
  transfers between devices with their start and end apart: 4 -> 3, of which waited for: 4 -> 3; matrix products, arithmetic and copies ran while one was open for 2% -> 2% of each run, Pallas kernels for 0% -> 0%
where the time goes in v1:
time: 392 us; the launch traced here: 391 us
  waiting for transfers between devices  187 us (48%)
  blocking collectives  104 us (27%)
  matrix products  42.7 us (11%)
  local copies, waits for them, and re-layouts  32.8 us (8%)
  between operations  16.3 us (4%)
  other arithmetic  9.34 us (2%)
    unnamed x4, waiting for transfers between devices  90.3 us
    reduce_scatter x1, waiting for transfers between devices, on_device(): lax.psum_scatter(summed.astype(jnp.float32), 'expert', scatter_dimension=...  56.5 us
    all_gather x1, waiting for transfers between devices, on_device(): every = lax.all_gather(column, 'dp', axis=1, tiled=True)  39.7 us
    psum x1, blocking collectives, on_device(): loss_sum, token_total = lax.psum((local_loss, jnp.sum(weights)), 'expert')  29 us
    all_gather x1, blocking collectives, on_device(): column = lax.all_gather(mine, 'expert', axis=0, tiled=True)  24.1 us
    all_to_all x1, blocking collectives, swapped_in(): tiles = lax.all_to_all(tiles, axis, split_axis=0, concat_axis=0)  19.7 us
    unnamed x11, local copies, waits for them, and re-layouts  16.9 us
    all_gather x1, blocking collectives, on_device(): lax.all_gather(gate_values * weights[:, None], 'expert', axis=0, tiled=True)  15.9 us
  transfers between devices with their start and end apart: 3, of which 3 were waited for; matrix products, arithmetic and copies ran while one was open for 2% of the time, Pallas kernels for 0%

profile of v1, /device:TPU:1, one launch (start us, length us, event | category | flops | bytes accessed | tf_op | source)
XLA Modules:
  0.0 391.4 jit_solution(9866477094055461407)
XLA Ops:
  7.2 1.0 dynamic-slice_convert_fusion
  8.2 24.1 %all_gather.13 = bf16[2048,128]{1,0:T(8,128)(2,1)} all-gather(bf16[128,128]{1,0:T(8,128)(2,1)S(1)} %dynamic-slice_convert_fusion), channel_id=1, replica_groups=mesh['dp'=16,'expert'=16] {'expert'}, dimensions={0}, use_global_device_ids=true | all-gather | bytes 557056 | tf_op jit(solution)/shard_map/all_gather | solution.py:26
  32.4 0.0 reduce-scatter.7.cloned.1.call-start
  32.4 0.7 convert_element_type.41
  33.1 14.9 %all_gather.12 = s32[2048,8]{0,1:T(8,128)S(1)} all-gather(s32[128,8]{0,1:T(8,128)} %param.8), channel_id=1, replica_groups=mesh['dp'=16,'expert'=16] {'expert'}, dimensions={0}, use_global_device_ids=true | all-gather | bytes 69632 | tf_op jit(solution)/shard_map/all_gather | solution.py:28
  47.9 0.2 compare_reduce_fusion
  48.2 1.4 copy.37
  49.6 2.8 subtract_bitcast_fusion
  52.4 1.6 copy.39
  54.0 0.7 broadcast_multiply_fusion
  54.7 15.9 %all_gather.15 = f32[2048,8]{0,1:T(8,128)S(1)} all-gather(f32[128,8]{0,1:T(8,128)S(1)} %broadcast_multiply_fusion), channel_id=1, replica_groups=mesh['dp'=16,'expert'=16] {'expert'}, dimensions={0}, use_global_device_ids=true | all-gather | bytes 69632 | tf_op jit(solution)/shard_map/all_gather | solution.py:29
  70.6 0.2 fusion.17
  70.9 0.4 select_reduce_fusion
  71.3 39.7 %all-gather.2.cloned.1.call-done = bf16[2048,2048]{1,0:T(8,128)(2,1)} async-done(((bf16[2048,128]{1,0:T(8,128)(2,1)}), bf16[2048,2048]{1,0:T(8,128)(2,1)}) %all-gather.2.cloned.1.call-update) | async-done | bytes 8388624 | tf_op jit(solution)/shard_map/all_gather | solution.py:27
  111.0 8.9 %convert_bitcast_fusion = bf16[8,16,16,2048]{3,2,0,1:T(8,128)(2,1)} fusion(bf16[16,128,2048,1]{2,1,3,0:T(8,128)(2,1)} %bitcast.49, s32[16,8,128]{2,1,0:T(8,128)S(1)} %copy.39, pred[16,8,128]{2,1,0:T(8,128)(4,1)S(1)} %compare_bitcast_fusion), kind=kOutput, calls=%fused_computation.5 | convolution fusion | flops 1078460416 | bytes 16859136 | tf_op jit(solution)/shard_map/best,btf->ebsf/dot_general | solution.py:44
  119.9 8.4 %copy.40 = bf16[8,16,16,2048]{3,2,1,0:T(8,128)(2,1)} copy(bf16[8,16,16,2048]{3,2,0,1:T(8,128)(2,1)} %convert_bitcast_fusion) | data formatting | bytes 16777216 | tf_op jit(solution)/shard_map/convert_element_type | solution.py:49
  128.3 7.0 %fusion.24 = f32[8,256,96]{1,2,0:T(8,128)} fusion(bf16[8,256,2048]{2,1,0:T(8,128)(2,1)} %bitcast.43, bf16[8,96,2048]{2,1,0:T(8,128)(2,1)S(1)} %copy-done.3), kind=kOutput, calls=%fused_computation.36 | convolution fusion | flops 805306368 | bytes 12320768 | tf_op jit(solution)/shard_map/erd,efd->erf/dot_general | solution.py:51
  135.3 15.4 %fusion.7 = f32[8,256,2048]{2,1,0:T(8,128)} fusion(bf16[8,96,2048]{2,1,0:T(8,128)(2,1)S(1)} %copy-done, bf16[8,256,2048]{2,1,0:T(8,128)(2,1)} %bitcast.44, bf16[8,96,2048]{2,1,0:T(8,128)(2,1)} %param.12, f32[8,256,96]{1,2,0:T(8,128)} %fusion.24), kind=kOutput, calls=%fused_computation.8 | convolution fusion | flops 1611792384 | bytes 32243712 | tf_op jit(solution)/shard_map/erf,efd->erd/dot_general | solution.py:54
  150.7 11.4 %bitcast_convert_fusion = bf16[16,128,2048]{2,1,0:T(8,128)(2,1)} fusion(f32[8,16,16,2048]{3,2,1,0:T(8,128)} %bitcast.40, f32[8,16,16]{2,0,1:T(8,128)S(1)} %bitcast.47, s32[16,8,128]{2,1,0:T(8,128)S(1)} %copy.39, pred[16,8,128]{2,1,0:T(8,128)(4,1)S(1)} %compare_bitcast_fusion), kind=kOutput, calls=%fused_computation | convolution fusion | flops 1086849024 | bytes 25255936 | tf_op jit(solution)/shard_map/best,ebsf->btf/dot_general | solution.py:59
  162.1 12.3 %copy.46 = bf16[2048,2048]{0,1:T(8,128)(2,1)} copy(bf16[2048,2048]{1,0:T(8,128)(2,1)} %bitcast.42) | data formatting | bytes 16777216
  174.5 0.0 reduce-scatter.5.cloned.1.call-start
  174.5 90.3 %reduce-scatter.7.cloned.1.call-done = bf16[128,2048]{1,0:T(8,128)(2,1)} async-done(((bf16[2048,2048]{1,0:T(8,128)(2,1)}), bf16[128,2048]{1,0:T(8,128)(2,1)}) %reduce-scatter.7.cloned.1.call-update) | async-done | bytes 524304
  264.8 2.0 copy.47
  266.8 2.1 convert_element_type.45
  268.9 56.5 %reduce-scatter.5.cloned.1.call-done = f32[128,128]{1,0:T(8,128)} async-done(((f32[2048,128]{1,0:T(8,128)}), f32[128,128]{1,0:T(8,128)}) %reduce-scatter.5.cloned.1.call-update) | async-done | bytes 65552 | tf_op jit(solution)/shard_map/reduce_scatter | solution.py:63
  325.4 0.9 stack.2
  326.4 19.7 %all_to_all.5 = f32[16,128,128]{2,1,0:T(8,128)} all-to-all(f32[16,128,128]{2,1,0:T(8,128)S(1)} %stack.2), channel_id=1, replica_groups=mesh['dp'=16,'expert'=16] {'dp'}, dimensions={0} | all-to-all | bytes 2097152 | tf_op jit(solution)/shard_map/all_to_all | solution.py:12
  346.1 2.6 copy.42
  348.6 1.5 fusion.8
  350.2 0.7 convert_reduce_fusion
  350.8 2.5 copy.43
  353.4 29.0 %all-reduce = (f32[]{:T(128)}, f32[]{:T(128)}) all-reduce(f32[]{:T(128)} %get-tuple-element.7, f32[]{:T(128)} %get-tuple-element.6), channel_id=1, replica_groups=mesh['dp'=16,'expert'=16] {'expert'}, use_global_device_ids=true, to_apply=%region_8.9 | all-reduce | flops 2 | bytes 16 | tf_op jit(solution)/shard_map/psum | solution.py:67
  (15 shorter events, 0.1 us)
Async XLA Ops:
  7.2 128.2 %copy-start = (bf16[8,96,2048]{2,1,0:T(8,128)(2,1)S(1)}, bf16[8,96,2048]{2,1,0:T(8,128)(2,1)}, u32[]{:S(2)}) copy-start(bf16[8,96,2048]{2,1,0:T(8,128)(2,1)} %param.13) | copy-start | bytes 9437188
  7.2 103.8 %all-gather.2.cloned.1.call-start = ((), (), s32[]{:S(2)}) async-start(), calls=%async_computation.3 | async-start | bytes 8912896 | tf_op jit(solution)/shard_map/all_gather | solution.py:27
  32.4 232.4 %reduce-scatter.7.cloned.1.call-start = ((), (), s32[]{:S(2)}) async-start(), calls=%async_computation.5 | async-start | bytes 8912896
  119.9 8.4 %copy-start.3 = (bf16[8,96,2048]{2,1,0:T(8,128)(2,1)S(1)}, bf16[8,96,2048]{2,1,0:T(8,128)(2,1)}, u32[]{:S(2)}) copy-start(bf16[8,96,2048]{2,1,0:T(8,128)(2,1)} %param.11) | copy-start | bytes 9437188
  174.5 209.3 %copy-start.1 = (bf16[8,96,2048]{2,1,0:T(8,128)(2,1)S(1)}, bf16[8,96,2048]{2,1,0:T(8,128)(2,1)}, u32[]{:S(2)}) copy-start(bf16[8,96,2048]{2,1,0:T(8,128)(2,1)} %param.13) | copy-start | bytes 9437188
  174.5 175.7 %copy-start.2 = (s32[128]{0:T(128)S(1)}, s32[128]{0:T(128)}, u32[]{:S(2)}) copy-start(s32[128]{0:T(128)} %param.10) | copy-start | bytes 1540
  174.5 150.9 %reduce-scatter.5.cloned.1.call-start = ((), (), s32[]{:S(2)}) async-start(), calls=%async_computation.4 | async-start | bytes 1114112 | tf_op jit(solution)/shard_map/reduce_scatter | solution.py:63
Sparse Core Ops, SparseCore 0:
  32.5 78.4 all-gather.1
  174.6 90.1 reduce-scatter.6
  269.1 56.2 reduce-scatter.4
